TPU v7x, 256 devices: a whole 4x4x8 slice. The times are simulated.
256 devices in a mesh: row: 8 (over x, core), col: 32 (over y, z).
Axes of the slice: x: 4, y: 4, z: 8, core: 2. Of those that a mesh axis runs over, the one named last changes fastest.
Arguments:
- hidden: bfloat16 [128, 8192], P('col', 'row'), may hold values from -6 to 6
- w_gate: bfloat16 [8192, 16384], P('row', 'col'), may hold values from -0.0625 to 0.0625
- w_up: bfloat16 [8192, 16384], P('row', 'col'), may hold values from -0.0625 to 0.0625
- prior: float32 [16384, 16384], P('row', 'col'), may hold values from -1 to 12, as said below
- rhs: float32 [16384, 4096], P('row', 'col'), may hold values from -6 to 6
Outputs:
- factored: float32 [16384, 16384], P('row', 'col')
- right_out: float32 [16384, 4096], P('row', 'col')
Inputs may be any that keep to these rules, and one draw needn't show every extreme that they name: prior is symmetric and positive definite, with smallest eigenvalue 0.1 or more.
All inputs are finite; a program needn't handle non-finite values.
Results may differ from a plain program's by a relative error of at most 0.0003.
Values may be sent and summed in bfloat16 or wider, within the bound.
No kernel may reach another device: no remote copies, remote signals or barrier semaphores. Data moves between devices by JAX's collectives and lax.ppermute only.
A program may use at most 64 MiB of HBM per device.

v0:
```python
import jax
import jax.numpy as jnp
from jax import lax
from jax.sharding import Mesh
from jax.sharding import PartitionSpec as P

P_SIZE = 128
PANELS = 2
COL = ("col_0", "col_1")
DAMP = 0.5


def joined_along(blocks, dim):
    blocks = jnp.moveaxis(blocks, 0, dim)
    lengths = blocks.shape
    return blocks.reshape(*lengths[:dim], lengths[dim] * lengths[dim + 1], *lengths[dim + 2 :])


def copy_for_each(shard, axis):
    peers = lax.axis_size(axis)
    return lax.all_to_all(
        jnp.broadcast_to(shard[None], (peers, *shard.shape)), axis, 0, 0, tiled=True
    )


def gathered_copies(shard, axis, dim):
    return joined_along(copy_for_each(shard, axis), dim)


def side_by_side(arrays, axis, dim, along):
    both = jnp.concatenate(arrays, axis=along)
    result, at, finished = (lax.psum_scatter(both, axis, scatter_dimension=dim, tiled=True), 0, [])
    for a in arrays:
        finished.append(lax.slice_in_dim(result, at, at + a.shape[along], axis=along))
        at += a.shape[along]
    return tuple(finished)


def spread(shard, axes, root):
    shard = jnp.where(lax.axis_index(axes) == root, shard, jnp.zeros_like(shard))
    for axis in axes:
        shard = lax.psum(shard, axis)
    return shard


def broadcast(shard, axis, root):
    return lax.dynamic_index_in_dim(lax.all_gather(shard, axis), root, 0, keepdims=False)


def local(hidden, w_gate, w_up, prior, rhs):
    rows_count = lax.axis_size("row")
    cols_count = lax.axis_size(COL)
    row_id = lax.axis_index("row")
    col_id = lax.axis_index(COL)
    ratio = cols_count // rows_count
    height, width = prior.shape
    tokens = gathered_copies(hidden, COL, 0)
    gate_part = jnp.dot(tokens, w_gate, preferred_element_type=jnp.float32)
    up_part = jnp.dot(tokens, w_up, preferred_element_type=jnp.float32)
    gate, upward = side_by_side((gate_part, up_part), "row", 0, 1)
    keys = gathered_copies(jax.nn.silu(gate) * upward, "row", 0)
    samples = keys.shape[0]
    regrouped = lax.all_to_all(keys, COL, split_axis=0, concat_axis=1, tiled=True)
    own_part = lax.dynamic_slice_in_dim(regrouped, row_id * height, height, 1)
    row_keys = gathered_copies(own_part, COL, 0)
    row_global = row_id * height + lax.iota(jnp.int32, height)
    col_global = col_id * width + lax.iota(jnp.int32, width)
    outer = lax.dot_general(
        row_keys,
        keys,
        (((0,), (0,)), ((), ())),
        precision=lax.Precision.HIGHEST,
        preferred_element_type=jnp.float32,
    )
    work = prior + outer / samples
    work = work + jnp.where(row_global[:, None] == col_global[None, :], DAMP, 0.0).astype(
        jnp.float32
    )
    right = rhs
    offsets = lax.iota(jnp.int32, P_SIZE)
    for panel in range(PANELS):
        start = panel * P_SIZE
        stop = start + P_SIZE
        column = spread(work[:, start:stop], COL, 0)
        pivot = jnp.linalg.cholesky(broadcast(column[start:stop], "row", 0))
        solved = jax.scipy.linalg.solve_triangular(pivot, column.T, lower=True).T
        placed = jnp.zeros_like(solved).at[start:stop].set(pivot)
        in_pivot = (row_global >= start) & (row_global < stop)
        beyond = row_global >= stop
        factor_cols = jnp.where(in_pivot[:, None], placed, jnp.where(beyond[:, None], solved, 0.0))
        matching = lax.dynamic_slice_in_dim(factor_cols, col_id % ratio * width, width, 0)
        across = broadcast(matching, "row", col_id // ratio)
        lower_rows = jnp.where(beyond[:, None], factor_cols, 0.0)
        upper_cols = jnp.where((col_global >= stop)[:, None], across, 0.0)
        work = work - lax.dot_general(
            lower_rows,
            upper_cols,
            (((1,), (1,)), ((), ())),
            precision=lax.Precision.HIGHEST,
            preferred_element_type=jnp.float32,
        )
        solution = jax.scipy.linalg.solve_triangular(
            factor_cols[start:stop], right[start:stop], lower=True
        )
        solution = broadcast(solution, "row", 0)
        right = right - jnp.dot(
            lower_rows,
            solution,
            precision=lax.Precision.HIGHEST,
            preferred_element_type=jnp.float32,
        )
        right = right.at[start:stop].set(jnp.where(row_id == 0, solution, right[start:stop]))
        keep_factor = (row_global[:, None] >= start + offsets[None, :]) & (col_id == 0)
        work = work.at[:, start:stop].set(jnp.where(keep_factor, factor_cols, work[:, start:stop]))
    return (work, right)


def solution(mesh):
    finer = Mesh(mesh.devices.reshape(mesh.shape["row"], 4, 8), ("row", "col_0", "col_1"))
    placed = (P(COL, "row"), P("row", COL), P("row", COL), P("row", COL), P("row", COL))
    return jax.shard_map(
        local,
        mesh=finer,
        in_specs=placed,
        out_specs=(P("row", COL), P("row", COL)),
        check_vma=False,
    )
```

profile of v0, /device:TPU:1, one launch (start us, length us, event | category | flops | bytes accessed | tf_op | source)
XLA Modules:
  0.0 588.0 jit_solution(16554936312668972503)
XLA Ops:
  8.1 21.5 %all_to_all.34 = bf16[32,4,1024]{2,1,0:T(4,128)(2,1)S(1)} all-to-all(bf16[32,4,1024]{2,1,0:T(4,128)(2,1)S(1)} %broadcast_in_dim.100), channel_id=1, replica_groups=mesh['row'=8,'col_0'=4,'col_1'=8] {'col_0','col_1'}, dimensions={0} | all-to-all | bytes 524288 | tf_op jit(solution)/shard_map/all_to_all | solution.py:21
  32.4 30.2 %reduce-scatter.2.cloned.1.call-done = f32[16,1024]{1,0:T(8,128)} async-done(((f32[128,1024]{1,0:T(8,128)}), f32[16,1024]{1,0:T(8,128)}) %reduce-scatter.2.cloned.1.call-update) | async-done | bytes 65552 | tf_op jit(solution)/shard_map/reduce_scatter | solution.py:32
  63.4 11.9 %all_to_all.35 = f32[8,16,512]{2,1,0:T(8,128)S(1)} all-to-all(f32[8,16,512]{2,1,0:T(8,128)S(1)} %broadcast_in_dim.101), channel_id=1, replica_groups=mesh['row'=8,'col_0'=4,'col_1'=8] {'row'}, dimensions={0} | all-to-all | bytes 524288 | tf_op jit(solution)/shard_map/all_to_all | solution.py:21
  76.0 9.6 %all-to-all-start.2 = ((f32[32,4,512]{2,1,0:T(4,128)}), f32[32,4,512]{2,1,0:T(4,128)S(1)}, u32[]{:S(2)}, u32[]{:S(2)}) async-start(f32[32,4,512]{2,1,0:T(4,128)} %all_to_all.25), calls=%async_computation.3 | async-start | bytes 524288 | tf_op jit(solution)/shard_map/all_to_all | solution.py:63
  85.6 9.7 %all-to-all-done.2 = f32[32,4,512]{2,1,0:T(4,128)S(1)} async-done(((f32[32,4,512]{2,1,0:T(4,128)}), f32[32,4,512]{2,1,0:T(4,128)S(1)}, u32[]{:S(2)}, u32[]{:S(2)}) %all-to-all-start.2) | async-done | bytes 262176 | tf_op jit(solution)/shard_map/all_to_all | solution.py:63
  96.5 6.0 %all-to-all-start.3 = ((f32[32,4,2048]{2,1,0:T(4,128)}), f32[32,4,2048]{2,1,0:T(4,128)S(1)}, u32[]{:S(2)}, u32[]{:S(2)}) async-start(f32[32,4,2048]{2,1,0:T(4,128)} %broadcast_in_dim.102), calls=%async_computation.4 | async-start | bytes 2097152 | tf_op jit(solution)/shard_map/all_to_all | solution.py:21
  102.6 24.3 %all-to-all-done.3 = f32[32,4,2048]{2,1,0:T(4,128)S(1)} async-done(((f32[32,4,2048]{2,1,0:T(4,128)}), f32[32,4,2048]{2,1,0:T(4,128)S(1)}, u32[]{:S(2)}, u32[]{:S(2)}) %all-to-all-start.3) | async-done | bytes 1048608 | tf_op jit(solution)/shard_map/all_to_all | solution.py:21
  127.3 5.8 select_add_fusion
  133.1 2.0 copy-done.2
  136.3 48.9 %all-reduce.7.cloned.1.call-done = f32[2048,128]{1,0:T(8,128)} async-done(((f32[2048,128]{1,0:T(8,128)}), f32[2048,128]{1,0:T(8,128)}) %all-reduce.7.cloned.1.call-update) | async-done | bytes 1048592 | tf_op jit(solution)/shard_map/psum | solution.py:42
  185.3 76.3 %all-reduce.9.cloned.1.call-done = f32[2048,128]{1,0:T(8,128)} async-done(((f32[2048,128]{1,0:T(8,128)}), f32[2048,128]{1,0:T(8,128)}) %all-reduce.9.cloned.1.call-update) | async-done | bytes 1048592 | tf_op jit(solution)/shard_map/psum | solution.py:42
  262.5 18.2 %all-gather = f32[1024,128]{1,0:T(8,128)S(1)} all-gather(f32[128,128]{1,0:T(8,128)S(1)} %slice.179), channel_id=2, replica_groups=mesh['row'=8,'col_0'=4,'col_1'=8] {'row'}, dimensions={0}, use_global_device_ids=true | all-gather | bytes 589824 | tf_op jit(solution)/shard_map/all_gather | solution.py:47
  280.9 11.7 %cholesky.44 = f32[128,128]{1,0:T(8,128)S(1)} custom-call(f32[128,128]{1,0:T(8,128)S(1)} %copy.8), custom_call_target="Cholesky" | custom-call | tf_op jit(solution)/shard_map/jit(cholesky)/cholesky | solution.py:85
  294.0 9.8 %custom-call.10 = f32[1,128,128]{1,2,0:T(8,128)S(1)} custom-call(f32[1,128,128]{2,1,0:T(8,128)S(1)} %get-tuple-element.79), custom_call_target="InvertDiagBlocksLowerTriangular" | custom-call | tf_op jit(solution)/shard_map/jit(_solve_triangular)/triangular_solve | solution.py:86
  303.8 3.3 fusion.3
  308.5 24.7 %all-gather.9.cloned.1.call-done = f32[4096,128]{1,0:T(8,128)} async-done(((f32[512,128]{1,0:T(8,128)}), f32[4096,128]{1,0:T(8,128)}) %all-gather.9.cloned.1.call-update) | async-done | bytes 2097168 | tf_op jit(solution)/shard_map/all_gather | solution.py:47
  333.3 5.5 convolution_subtract_fusion.1
  339.9 2.0 copy-done.1
  343.1 49.5 %all-reduce.11.cloned.1.call-done = f32[2048,128]{1,0:T(8,128)} async-done(((f32[2048,128]{1,0:T(8,128)}), f32[2048,128]{1,0:T(8,128)}) %all-reduce.11.cloned.1.call-update) | async-done | bytes 1048592 | tf_op jit(solution)/shard_map/psum | solution.py:42
  392.7 76.3 %all-reduce.13.cloned.1.call-done = f32[2048,128]{1,0:T(8,128)} async-done(((f32[2048,128]{1,0:T(8,128)}), f32[2048,128]{1,0:T(8,128)}) %all-reduce.13.cloned.1.call-update) | async-done | bytes 1048592 | tf_op jit(solution)/shard_map/psum | solution.py:42
  469.9 18.3 %all-gather.2 = f32[1024,128]{1,0:T(8,128)S(1)} all-gather(f32[128,128]{1,0:T(8,128)S(1)} %slice.183), channel_id=4, replica_groups=mesh['row'=8,'col_0'=4,'col_1'=8] {'row'}, dimensions={0}, use_global_device_ids=true | all-gather | bytes 589824 | tf_op jit(solution)/shard_map/all_gather | solution.py:47
  488.3 11.7 %cholesky.55 = f32[128,128]{1,0:T(8,128)S(1)} custom-call(f32[128,128]{1,0:T(8,128)S(1)} %copy.11), custom_call_target="Cholesky" | custom-call | tf_op jit(solution)/shard_map/jit(cholesky)/cholesky | solution.py:85
  501.4 9.8 %custom-call.11 = f32[1,128,128]{1,2,0:T(8,128)S(1)} custom-call(f32[1,128,128]{2,1,0:T(8,128)S(1)} %get-tuple-element.77), custom_call_target="InvertDiagBlocksLowerTriangular" | custom-call | tf_op jit(solution)/shard_map/jit(_solve_triangular)/triangular_solve | solution.py:86
  511.2 3.2 fusion.1
  515.9 9.8 %custom-call.12 = f32[1,128,128]{1,2,0:T(8,128)S(1)} custom-call(f32[1,128,128]{2,1,0:T(8,128)S(1)} %fusion.32), custom_call_target="InvertDiagBlocksLowerTriangular" | custom-call | tf_op jit(solution)/shard_map/jit(_solve_triangular)/triangular_solve | solution.py:102
  526.9 14.2 %all-gather.4 = f32[1024,128]{1,0:T(8,128)S(1)} all-gather(f32[128,128]{1,0:T(8,128)S(1)} %fusion.34), channel_id=6, replica_groups=mesh['row'=8,'col_0'=4,'col_1'=8] {'row'}, dimensions={0}, use_global_device_ids=true | all-gather | bytes 589824 | tf_op jit(solution)/shard_map/all_gather | solution.py:47
  541.1 3.1 convolution_subtract_fusion.3
  545.7 9.8 %custom-call.13 = f32[1,128,128]{1,2,0:T(8,128)S(1)} custom-call(f32[1,128,128]{2,1,0:T(8,128)S(1)} %fusion.30), custom_call_target="InvertDiagBlocksLowerTriangular" | custom-call | tf_op jit(solution)/shard_map/jit(_solve_triangular)/triangular_solve | solution.py:102
  556.6 13.1 %all-gather.5 = f32[1024,128]{1,0:T(8,128)S(1)} all-gather(f32[128,128]{1,0:T(8,128)S(1)} %fusion.28), channel_id=7, replica_groups=mesh['row'=8,'col_0'=4,'col_1'=8] {'row'}, dimensions={0}, use_global_device_ids=true | all-gather | bytes 589824 | tf_op jit(solution)/shard_map/all_gather | solution.py:47
  569.8 2.3 convolution_subtract_fusion.2
  572.1 5.9 %convolution_subtract_fusion = f32[2048,512]{1,0:T(8,128)S(1)} fusion(f32[2048,512]{1,0:T(8,128)} %copy-done.1, f32[2048,128]{1,0:T(8,128)S(1)} %fusion.1, pred[2048]{0:T(1024)(128)(4,1)S(1)} %fusion.44, f32[8,512,128]{2,1,0:T(8,128)} %bitcast.62, s32[]{:T(128)S(6)} %select_n.113, pred[512]{0:T(512)(128)(4,1)S(1)} %fusion.52), kind=kOutput, calls=%fused_computation.1 | convolution fusion | flops 1611988992 | bytes 9701892 | tf_op jit(solution)/shard_map/dot_general | solution.py:95
  579.1 2.0 copy-done.3
  (71 shorter events, 22.9 us)
Async XLA Ops:
  7.2 22.5 %copy-start = (bf16[1024,512]{1,0:T(8,128)(2,1)S(1)}, bf16[1024,512]{1,0:T(8,128)(2,1)}, u32[]{:S(2)}) copy-start(bf16[1024,512]{1,0:T(8,128)(2,1)} %param.23) | copy-start | bytes 3145732
  7.2 55.4 %reduce-scatter.2.cloned.1.call-start = ((), (), s32[]{:S(2)}) async-start(), calls=%async_computation.5 | async-start | bytes 589824 | tf_op jit(solution)/shard_map/reduce_scatter | solution.py:32
  76.0 19.2 %all-to-all-start.2 = ((f32[32,4,512]{2,1,0:T(4,128)}), f32[32,4,512]{2,1,0:T(4,128)S(1)}, u32[]{:S(2)}, u32[]{:S(2)}) async-start(f32[32,4,512]{2,1,0:T(4,128)} %all_to_all.25), calls=%async_computation.3 | async-start | bytes 524288 | tf_op jit(solution)/shard_map/all_to_all | solution.py:63
  96.5 30.5 %all-to-all-start.3 = ((f32[32,4,2048]{2,1,0:T(4,128)}), f32[32,4,2048]{2,1,0:T(4,128)S(1)}, u32[]{:S(2)}, u32[]{:S(2)}) async-start(f32[32,4,2048]{2,1,0:T(4,128)} %broadcast_in_dim.102), calls=%async_computation.4 | async-start | bytes 2097152 | tf_op jit(solution)/shard_map/all_to_all | solution.py:21
  102.6 82.6 %all-reduce.7.cloned.1.call-start = ((), (), s32[]{:S(2)}) async-start(), calls=%async_computation.6 | async-start | bytes 2097152 | tf_op jit(solution)/shard_map/psum | solution.py:42
  133.1 2.0 copy-start.2
  136.3 125.4 %all-reduce.9.cloned.1.call-start = ((), (), s32[]{:S(2)}) async-start(), calls=%async_computation.7 | async-start | bytes 2097152 | tf_op jit(solution)/shard_map/psum | solution.py:42
  185.2 148.1 %all-gather.9.cloned.1.call-start = ((), (), s32[]{:S(2)}) async-start(), calls=%async_computation.10 | async-start | bytes 2359296 | tf_op jit(solution)/shard_map/all_gather | solution.py:47
  307.8 84.8 %all-reduce.11.cloned.1.call-start = ((), (), s32[]{:S(2)}) async-start(), calls=%async_computation.8 | async-start | bytes 2097152 | tf_op jit(solution)/shard_map/psum | solution.py:42
  339.9 2.0 copy-start.1
  343.0 126.0 %all-reduce.13.cloned.1.call-start = ((), (), s32[]{:S(2)}) async-start(), calls=%async_computation.9 | async-start | bytes 2097152 | tf_op jit(solution)/shard_map/psum | solution.py:42
  392.6 179.5 %all-gather.11.cloned.1.call-start = ((), (), s32[]{:S(2)}) async-start(), calls=%async_computation.11 | async-start | bytes 2359296 | tf_op jit(solution)/shard_map/all_gather | solution.py:47
  572.1 5.9 %copy-start.4 = (f32[2048,128]{1,0:T(8,128)}, f32[2048,128]{1,0:T(8,128)S(1)}, u32[]{:S(2)}) copy-start(f32[2048,128]{1,0:T(8,128)S(1)} %fusion.27) | copy-start | bytes 3145732
  579.1 2.0 copy-start.3
Sparse Core Ops, SparseCore 0:
  32.5 29.9 reduce-scatter.1
  136.4 48.7 all-reduce.6
  187.5 74.0 all-reduce.8
  307.9 25.3 all-gather.8
  343.1 49.4 all-reduce.10
  394.9 74.0 all-reduce.12
  515.4 26.1 all-gather.10
where the time goes:
time: 589 us; the launch traced here: 588 us
  waiting for transfers between devices  340 us (58%)
  blocking collectives  97.3 us (17%)
  other arithmetic  74.2 us (13%)
  matrix products  33.2 us (6%)
  starting transfers between devices  15.9 us (3%)
  between operations  14.5 us (2%)
  local copies, waits for them, and re-layouts  12.9 us (2%)
    psum x4, waiting for transfers between devices, spread(): shard = lax.psum(shard, axis)  251 us
    all_gather x4, blocking collectives, broadcast(): lax.all_gather(shard, axis)  63.8 us
    all_to_all x2, blocking collectives, copy_for_each(): lax.all_to_all(jnp.broadcast_to(shard[None], (peers, *shard.shape)), axis...  33.4 us
    reduce_scatter x1, waiting for transfers between devices, side_by_side(): lax.psum_scatter(both, axis, scatter_dimension=dim, tiled=True)  30.2 us
    another operation x6, other arithmetic, local(): pivot = jnp.linalg.cholesky(broadcast(column[start:stop], 'row', 0))  24.8 us
    all_gather x2, waiting for transfers between devices, broadcast(): lax.all_gather(shard, axis)  24.7 us
    all_to_all x1, waiting for transfers between devices, copy_for_each(): lax.all_to_all(jnp.broadcast_to(shard[None], (peers, *shard.shape)), axis...  24.3 us
    another operation x4, other arithmetic, local(): solved = jax.scipy.linalg.solve_triangular(pivot, column.T, lower=True).T  20.9 us
  transfers between devices with their start and end apart: 9, of which 8 were waited for; matrix products, arithmetic and copies ran while one was open for 5% of the time, Pallas kernels for 0%

commit v1 on v0

--- a/solution.py
+++ b/solution.py
@@ -39,7 +39,7 @@
 def spread(shard, axes, root):
     shard = jnp.where(lax.axis_index(axes) == root, shard, jnp.zeros_like(shard))
     for axis in axes:
-        shard = lax.psum(shard, axis)
+        shard = jnp.sum(lax.all_gather(shard, axis), axis=0)
     return shard
 
 

time: 589 us -> 626 us (1.063)
  waiting for transfers between devices: 340 us -> 380 us
  other arithmetic: 74.2 us -> 89 us
  blocking collectives: 97.3 us -> 88.9 us
  matrix products: 33.2 us -> 26.5 us
    all_gather x0 -> x4, waiting for transfers between devices: none -> 290 us  [spread(): shard = jnp.sum(lax.all_gather(shard, axis), axis=0)]
    psum x4 -> x0, waiting for transfers between devices: 251 us -> none  [spread(): shard = lax.psum(shard, axis)]
    reduce_sum x0 -> x4, other arithmetic: none -> 14.8 us  [spread(): shard = jnp.sum(lax.all_gather(shard, axis), axis=0)]
    all_gather x4, blocking collectives: 63.8 us -> 55.5 us  [broadcast(): lax.all_gather(shard, axis)]
where the time goes in v1:
time: 626 us
  waiting for transfers between devices  380 us (61%)
  other arithmetic  89 us (14%)
  blocking collectives  88.9 us (14%)
  matrix products  26.5 us (4%)
  starting transfers between devices  15.8 us (3%)
  between operations  14.5 us (2%)
  local copies, waits for them, and re-layouts  11.2 us (2%)
    all_gather x4, waiting for transfers between devices, spread(): shard = jnp.sum(lax.all_gather(shard, axis), axis=0)  290 us
    all_gather x4, blocking collectives, broadcast(): lax.all_gather(shard, axis)  55.5 us
    all_to_all x2, blocking collectives, copy_for_each(): lax.all_to_all(jnp.broadcast_to(shard[None], (peers, *shard.shape)), axis...  33.4 us
    reduce_scatter x1, waiting for transfers between devices, side_by_side(): lax.psum_scatter(both, axis, scatter_dimension=dim, tiled=True)  30.2 us
    all_gather x2, waiting for transfers between devices, broadcast(): lax.all_gather(shard, axis)  25 us
    another operation x6, other arithmetic, local(): pivot = jnp.linalg.cholesky(broadcast(column[start:stop], 'row', 0))  24.8 us
    all_to_all x1, waiting for transfers between devices, copy_for_each(): lax.all_to_all(jnp.broadcast_to(shard[None], (peers, *shard.shape)), axis...  24.3 us
    another operation x4, other arithmetic, local(): solved = jax.scipy.linalg.solve_triangular(pivot, column.T, lower=True).T  20.9 us
  transfers between devices with their start and end apart: 9, of which 8 were waited for; matrix products, arithmetic and copies ran while one was open for 5% of the time, Pallas kernels for 0%

profile of v1, /device:TPU:1, one launch (start us, length us, event | category | flops | bytes accessed | tf_op | source)
XLA Modules:
  0.0 625.5 jit_solution(7888110909538426722)
XLA Ops:
  8.1 21.5 %all_to_all.34 = bf16[32,4,1024]{2,1,0:T(4,128)(2,1)S(1)} all-to-all(bf16[32,4,1024]{2,1,0:T(4,128)(2,1)S(1)} %broadcast_in_dim.100), channel_id=1, replica_groups=mesh['row'=8,'col_0'=4,'col_1'=8] {'col_0','col_1'}, dimensions={0} | all-to-all | bytes 524288 | tf_op jit(solution)/shard_map/all_to_all | solution.py:21
  32.4 30.2 %reduce-scatter.2.cloned.1.call-done = f32[16,1024]{1,0:T(8,128)} async-done(((f32[128,1024]{1,0:T(8,128)}), f32[16,1024]{1,0:T(8,128)}) %reduce-scatter.2.cloned.1.call-update) | async-done | bytes 65552 | tf_op jit(solution)/shard_map/reduce_scatter | solution.py:32
  63.5 11.9 %all_to_all.35 = f32[8,16,512]{2,1,0:T(8,128)S(1)} all-to-all(f32[8,16,512]{2,1,0:T(8,128)S(1)} %broadcast_in_dim.101), channel_id=1, replica_groups=mesh['row'=8,'col_0'=4,'col_1'=8] {'row'}, dimensions={0} | all-to-all | bytes 524288 | tf_op jit(solution)/shard_map/all_to_all | solution.py:21
  76.1 9.5 %all-to-all-start.2 = ((f32[32,4,512]{2,1,0:T(4,128)}), f32[32,4,512]{2,1,0:T(4,128)S(1)}, u32[]{:S(2)}, u32[]{:S(2)}) async-start(f32[32,4,512]{2,1,0:T(4,128)} %all_to_all.25), calls=%async_computation.3 | async-start | bytes 524288 | tf_op jit(solution)/shard_map/all_to_all | solution.py:63
  85.6 9.7 %all-to-all-done.2 = f32[32,4,512]{2,1,0:T(4,128)S(1)} async-done(((f32[32,4,512]{2,1,0:T(4,128)}), f32[32,4,512]{2,1,0:T(4,128)S(1)}, u32[]{:S(2)}, u32[]{:S(2)}) %all-to-all-start.2) | async-done | bytes 262176 | tf_op jit(solution)/shard_map/all_to_all | solution.py:63
  96.5 6.0 all-to-all-start.3
  102.6 24.3 %all-to-all-done.3 = f32[32,4,2048]{2,1,0:T(4,128)S(1)} async-done(((f32[32,4,2048]{2,1,0:T(4,128)}), f32[32,4,2048]{2,1,0:T(4,128)S(1)}, u32[]{:S(2)}, u32[]{:S(2)}) %all-to-all-start.3) | async-done | bytes 1048608 | tf_op jit(solution)/shard_map/all_to_all | solution.py:21
  127.3 5.8 select_add_fusion
  136.3 50.2 %all-gather.17.cloned.1.call-done = f32[8192,128]{1,0:T(8,128)} async-done(((f32[2048,128]{1,0:T(8,128)}), f32[8192,128]{1,0:T(8,128)}) %all-gather.17.cloned.1.call-update) | async-done | bytes 4194320 | tf_op jit(solution)/shard_map/all_gather | solution.py:42
  186.5 3.5 reduce_sum.36
  190.1 94.6 %all-gather.19.cloned.1.call-done = f32[16384,128]{1,0:T(8,128)} async-done(((f32[2048,128]{1,0:T(8,128)}), f32[16384,128]{1,0:T(8,128)}) %all-gather.19.cloned.1.call-update) | async-done | bytes 8388624 | tf_op jit(solution)/shard_map/all_gather | solution.py:42
  284.6 3.9 reduce_sum.37
  288.6 14.1 %all-gather.2 = f32[1024,128]{0,1:T(8,128)S(1)} all-gather(f32[128,128]{0,1:T(8,128)S(1)} %copy.19), channel_id=4, replica_groups=mesh['row'=8,'col_0'=4,'col_1'=8] {'row'}, dimensions={0}, use_global_device_ids=true | all-gather | bytes 589824 | tf_op jit(solution)/shard_map/all_gather | solution.py:47
  302.9 11.7 %cholesky.44 = f32[128,128]{1,0:T(8,128)S(1)} custom-call(f32[128,128]{1,0:T(8,128)S(1)} %fusion.39), custom_call_target="Cholesky" | custom-call | tf_op jit(solution)/shard_map/jit(cholesky)/cholesky | solution.py:85
  315.9 9.8 %custom-call.10 = f32[1,128,128]{1,2,0:T(8,128)S(1)} custom-call(f32[1,128,128]{2,1,0:T(8,128)S(1)} %get-tuple-element.79), custom_call_target="InvertDiagBlocksLowerTriangular" | custom-call | tf_op jit(solution)/shard_map/jit(_solve_triangular)/triangular_solve | solution.py:86
  328.3 25.0 %all-gather.21.cloned.1.call-done = f32[4096,128]{1,0:T(8,128)} async-done(((f32[512,128]{1,0:T(8,128)}), f32[4096,128]{1,0:T(8,128)}) %all-gather.21.cloned.1.call-update) | async-done | bytes 2097168 | tf_op jit(solution)/shard_map/all_gather | solution.py:47
  353.3 5.5 convolution_subtract_fusion.1
  359.9 2.0 copy-done.2
  363.1 50.9 %all-gather.23.cloned.1.call-done = f32[8192,128]{1,0:T(8,128)} async-done(((f32[2048,128]{1,0:T(8,128)}), f32[8192,128]{1,0:T(8,128)}) %all-gather.23.cloned.1.call-update) | async-done | bytes 4194320 | tf_op jit(solution)/shard_map/all_gather | solution.py:42
  414.0 3.5 reduce_sum.38
  417.6 94.6 %all-gather.25.cloned.1.call-done = f32[16384,128]{1,0:T(8,128)} async-done(((f32[2048,128]{1,0:T(8,128)}), f32[16384,128]{1,0:T(8,128)}) %all-gather.25.cloned.1.call-update) | async-done | bytes 8388624 | tf_op jit(solution)/shard_map/all_gather | solution.py:42
  512.1 3.9 reduce_sum.39
  516.1 14.1 %all-gather.6 = f32[1024,128]{0,1:T(8,128)S(1)} all-gather(f32[128,128]{0,1:T(8,128)S(1)} %copy.20), channel_id=8, replica_groups=mesh['row'=8,'col_0'=4,'col_1'=8] {'row'}, dimensions={0}, use_global_device_ids=true | all-gather | bytes 589824 | tf_op jit(solution)/shard_map/all_gather | solution.py:47
  530.4 11.7 %cholesky.55 = f32[128,128]{1,0:T(8,128)S(1)} custom-call(f32[128,128]{1,0:T(8,128)S(1)} %fusion.37), custom_call_target="Cholesky" | custom-call | tf_op jit(solution)/shard_map/jit(cholesky)/cholesky | solution.py:85
  543.5 9.8 %custom-call.11 = f32[1,128,128]{1,2,0:T(8,128)S(1)} custom-call(f32[1,128,128]{2,1,0:T(8,128)S(1)} %get-tuple-element.77), custom_call_target="InvertDiagBlocksLowerTriangular" | custom-call | tf_op jit(solution)/shard_map/jit(_solve_triangular)/triangular_solve | solution.py:86
  555.8 9.8 %custom-call.12 = f32[1,128,128]{1,2,0:T(8,128)S(1)} custom-call(f32[1,128,128]{2,1,0:T(8,128)S(1)} %fusion.32), custom_call_target="InvertDiagBlocksLowerTriangular" | custom-call | tf_op jit(solution)/shard_map/jit(_solve_triangular)/triangular_solve | solution.py:102
  566.7 14.1 %all-gather.8 = f32[1024,128]{1,0:T(8,128)S(1)} all-gather(f32[128,128]{1,0:T(8,128)S(1)} %fusion.34), channel_id=10, replica_groups=mesh['row'=8,'col_0'=4,'col_1'=8] {'row'}, dimensions={0}, use_global_device_ids=true | all-gather | bytes 589824 | tf_op jit(solution)/shard_map/all_gather | solution.py:47
  580.8 2.3 convolution_subtract_fusion.3
  583.2 9.8 %custom-call.13 = f32[1,128,128]{1,2,0:T(8,128)S(1)} custom-call(f32[1,128,128]{2,1,0:T(8,128)S(1)} %fusion.30), custom_call_target="InvertDiagBlocksLowerTriangular" | custom-call | tf_op jit(solution)/shard_map/jit(_solve_triangular)/triangular_solve | solution.py:102
  593.3 13.1 %all-gather.9 = f32[1024,128]{1,0:T(8,128)S(1)} all-gather(f32[128,128]{1,0:T(8,128)S(1)} %fusion.28), channel_id=11, replica_groups=mesh['row'=8,'col_0'=4,'col_1'=8] {'row'}, dimensions={0}, use_global_device_ids=true | all-gather | bytes 589824 | tf_op jit(solution)/shard_map/all_gather | solution.py:47
  606.4 2.0 convolution_subtract_fusion.2
  610.0 5.6 convolution_subtract_fusion
  (75 shorter events, 26.4 us)
Async XLA Ops:
  7.2 22.5 %copy-start = (bf16[1024,512]{1,0:T(8,128)(2,1)S(1)}, bf16[1024,512]{1,0:T(8,128)(2,1)}, u32[]{:S(2)}) copy-start(bf16[1024,512]{1,0:T(8,128)(2,1)} %param.23) | copy-start | bytes 3145732
  7.2 55.5 %reduce-scatter.2.cloned.1.call-start = ((), (), s32[]{:S(2)}) async-start(), calls=%async_computation.5 | async-start | bytes 589824 | tf_op jit(solution)/shard_map/reduce_scatter | solution.py:32
  76.1 19.2 %all-to-all-start.2 = ((f32[32,4,512]{2,1,0:T(4,128)}), f32[32,4,512]{2,1,0:T(4,128)S(1)}, u32[]{:S(2)}, u32[]{:S(2)}) async-start(f32[32,4,512]{2,1,0:T(4,128)} %all_to_all.25), calls=%async_computation.3 | async-start | bytes 524288 | tf_op jit(solution)/shard_map/all_to_all | solution.py:63
  96.5 30.5 %all-to-all-start.3 = ((f32[32,4,2048]{2,1,0:T(4,128)}), f32[32,4,2048]{2,1,0:T(4,128)S(1)}, u32[]{:S(2)}, u32[]{:S(2)}) async-start(f32[32,4,2048]{2,1,0:T(4,128)} %broadcast_in_dim.102), calls=%async_computation.4 | async-start | bytes 2097152 | tf_op jit(solution)/shard_map/all_to_all | solution.py:21
  102.6 83.9 %all-gather.17.cloned.1.call-start = ((), (), s32[]{:S(2)}) async-start(), calls=%async_computation.6 | async-start | bytes 5242880 | tf_op jit(solution)/shard_map/all_gather | solution.py:42
  133.1 2.0 copy-start.3
  136.3 148.4 %all-gather.19.cloned.1.call-start = ((), (), s32[]{:S(2)}) async-start(), calls=%async_computation.7 | async-start | bytes 9437184 | tf_op jit(solution)/shard_map/all_gather | solution.py:42
  190.0 163.3 %all-gather.21.cloned.1.call-start = ((), (), s32[]{:S(2)}) async-start(), calls=%async_computation.8 | async-start | bytes 2359296 | tf_op jit(solution)/shard_map/all_gather | solution.py:47
  327.5 86.5 %all-gather.23.cloned.1.call-start = ((), (), s32[]{:S(2)}) async-start(), calls=%async_computation.9 | async-start | bytes 5242880 | tf_op jit(solution)/shard_map/all_gather | solution.py:42
  359.9 2.0 copy-start.2
  363.0 149.1 %all-gather.25.cloned.1.call-start = ((), (), s32[]{:S(2)}) async-start(), calls=%async_computation.10 | async-start | bytes 9437184 | tf_op jit(solution)/shard_map/all_gather | solution.py:42
  417.5 192.5 %all-gather.27.cloned.1.call-start = ((), (), s32[]{:S(2)}) async-start(), calls=%async_computation.11 | async-start | bytes 2359296 | tf_op jit(solution)/shard_map/all_gather | solution.py:47
  610.0 8.7 %copy-start.1 = (bf16[1024,512]{1,0:T(8,128)(2,1)S(1)}, bf16[1024,512]{1,0:T(8,128)(2,1)}, u32[]{:S(2)}) copy-start(bf16[1024,512]{1,0:T(8,128)(2,1)} %param.23) | copy-start | bytes 3145732
  616.7 2.0 copy-start.4
Sparse Core Ops, SparseCore 0:
  32.5 30.0 reduce-scatter.1
  136.4 50.0 all-gather.16
  190.1 94.4 all-gather.18
  327.6 25.6 all-gather.20
  363.2 50.7 all-gather.22
  417.6 94.4 all-gather.24
  555.2 26.3 all-gather.26
